TPU v7x, 32 devices: a whole 2x2x4 slice. The times are simulated.
32 devices in a mesh: grp: 2 (over core), cores: 16 (over z, y, x).
Axes of the slice: x: 2, y: 2, z: 4, core: 2. Of those that a mesh axis runs over, the one named last changes fastest.
Arguments:
- rhs_core: float32 [4, 8192], P(None, 'cores'), may hold values from -6 to 6
- rhs_noncore: float32 [4, 8192], P(None, ('grp', 'cores')), may hold values from -6 to 6
- records_core: float32 [4, 8192], P(None, 'cores'), may hold values from 0.2 to 2
- records_noncore: float32 [4, 8192], P(None, ('grp', 'cores')), may hold values from 0.2 to 2
- core_inverse: bfloat16 [8192, 8192], P('cores'), as said below
- genomic_block: bfloat16 [8192, 8192], P(('grp', 'cores')), may hold values from -0.125 to 0.125
- m_inverse: float32 [8192], P(('grp', 'cores')), may hold values from 0.5 to 4
- trait_inverse: float32 [4, 4], replicated, as said below
Outputs:
- sol_core: float32 [4, 8192], P(None, 'cores')
- sol_noncore: float32 [4, 8192], P(None, ('grp', 'cores'))
- res_core: float32 [4, 8192], P(None, 'cores')
- res_noncore: float32 [4, 8192], P(None, ('grp', 'cores'))
Inputs may be any that keep to these rules, and one draw needn't show every extreme that they name: core_inverse is symmetric and positive definite. trait_inverse is symmetric and positive definite.
All inputs are finite; a program needn't handle non-finite values.
Results may differ from a plain program's by a relative error of at most 0.028.
Values may be sent and summed in bfloat16 or wider, within the bound.
No kernel may reach another device: no remote copies, remote signals or barrier semaphores. Data moves between devices by JAX's collectives and lax.ppermute only.
A program may use at most 64 MiB of HBM per device.

v0:
```python
import jax
import jax.numpy as jnp
from jax import lax
from jax.sharding import PartitionSpec as P

ITERS = 2


def genomic_map(core_vec, non_vec, core_inverse, genomic_block, m_inverse):
    core_in = core_vec.astype(jnp.bfloat16)
    partial_map = jnp.dot(core_in, core_inverse, preferred_element_type=jnp.float32)
    mapped = lax.psum(partial_map, "cores")
    mapped_in = mapped.astype(jnp.bfloat16)
    pulled = lax.dot_general(
        mapped_in, genomic_block, (((1,), (1,)), ((), ())), preferred_element_type=jnp.float32
    )
    scaled = m_inverse[None, :] * (non_vec - pulled)
    pushed_part = jnp.dot(
        scaled.astype(jnp.bfloat16), genomic_block, preferred_element_type=jnp.float32
    )
    grouped = lax.psum(pushed_part.astype(jnp.bfloat16), "grp")
    pushed = lax.psum_scatter(grouped, "cores", scatter_dimension=1, tiled=True).astype(jnp.float32)
    remainder = (core_vec - pushed).astype(jnp.bfloat16)
    back_part = jnp.dot(remainder, core_inverse, preferred_element_type=jnp.float32)
    core_out = lax.psum_scatter(
        back_part.astype(jnp.bfloat16), "cores", scatter_dimension=1, tiled=True
    ).astype(jnp.float32)
    return (core_out, scaled)


def body(
    rhs_core,
    rhs_noncore,
    records_core,
    records_noncore,
    core_inverse,
    genomic_block,
    m_inverse,
    trait_inverse,
):
    highest = lax.Precision.HIGHEST
    first_copy = (lax.axis_index("grp") == 0).astype(jnp.float32)
    trait_diag = jnp.diagonal(trait_inverse)[:, None]
    prec_core = 1.0 / (records_core + trait_diag)
    prec_non = 1.0 / (records_noncore + trait_diag * m_inverse[None, :])
    sol_core = jnp.zeros_like(rhs_core)
    sol_non = jnp.zeros_like(rhs_noncore)
    res_core, res_non = (rhs_core, rhs_noncore)
    z_core, z_non = (prec_core * res_core, prec_non * res_non)
    dir_core, dir_non = (z_core, z_non)

    def residual_inner(core_a, core_b, non_a, non_b):
        local_sum = jnp.sum(non_a * non_b) + first_copy * jnp.sum(core_a * core_b)
        return lax.psum(local_sum, ("grp", "cores"))

    rz_now = residual_inner(res_core, z_core, res_non, z_non)
    for iteration in range(ITERS):
        core_out, non_out = genomic_map(dir_core, dir_non, core_inverse, genomic_block, m_inverse)
        image_core = records_core * dir_core + jnp.dot(trait_inverse, core_out, precision=highest)
        image_non = records_noncore * dir_non + jnp.dot(trait_inverse, non_out, precision=highest)
        local_curve = jnp.sum(dir_non * image_non) + first_copy * jnp.sum(dir_core * image_core)
        step_size = rz_now / lax.psum(local_curve, ("grp", "cores"))
        sol_core = sol_core + step_size * dir_core
        sol_non = sol_non + step_size * dir_non
        res_core = res_core - step_size * image_core
        res_non = res_non - step_size * image_non
        if iteration + 1 < ITERS:
            z_core, z_non = (prec_core * res_core, prec_non * res_non)
            rz_next = residual_inner(res_core, z_core, res_non, z_non)
            factor = rz_next / rz_now
            dir_core = z_core + factor * dir_core
            dir_non = z_non + factor * dir_non
            rz_now = rz_next
    return (sol_core, sol_non, res_core, res_non)


def solution(mesh):
    in_specs = (
        P(None, "cores"),
        P(None, ("grp", "cores")),
        P(None, "cores"),
        P(None, ("grp", "cores")),
        P("cores", None),
        P(("grp", "cores"), None),
        P(("grp", "cores")),
        P(),
    )
    out_specs = (
        P(None, "cores"),
        P(None, ("grp", "cores")),
        P(None, "cores"),
        P(None, ("grp", "cores")),
    )
    return jax.shard_map(body, mesh=mesh, in_specs=in_specs, out_specs=out_specs, check_vma=False)
```

profile of v0, /device:TPU:12, one launch (start us, length us, event | category | flops | bytes accessed | tf_op | source)
XLA Modules:
  0.0 657.4 jit_solution(4603464972572962994)
XLA Ops:
  9.3 4.6 fusion.12
  13.9 67.9 %all-reduce.3 = bf16[4,8192]{1,0:T(4,128)(2,1)S(1)} all-reduce(f32[4,8192]{1,0:T(4,128)S(1)} %fusion.12), channel_id=1, replica_groups=mesh['grp'=2,'cores'=16] {'cores'}, use_global_device_ids=true, to_apply=%region_3.4 | all-reduce | flops 32768 | bytes 196608 | tf_op jit(solution)/shard_map/psum | solution.py:12
  81.9 3.5 fusion.5
  86.1 1.9 copy.16
  88.1 78.8 %reduce-scatter.17.cloned.1.call-done = bf16[512,4]{1,0:T(8,128)(2,1)} async-done(((bf16[8192,4]{1,0:T(8,128)(2,1)}), bf16[512,4]{1,0:T(8,128)(2,1)}) %reduce-scatter.17.cloned.1.call-update) | async-done | bytes 4112
  166.9 1.0 copy.17
  167.9 2.5 psum.64
  170.4 4.6 convolution_convert_fusion.2
  174.9 1.9 copy.12
  177.7 77.5 %reduce-scatter.13.cloned.1.call-done = bf16[512,4]{1,0:T(8,128)(2,1)} async-done(((bf16[8192,4]{1,0:T(8,128)(2,1)}), bf16[512,4]{1,0:T(8,128)(2,1)}) %reduce-scatter.13.cloned.1.call-update) | async-done | bytes 4112
  255.2 1.7 multiply_reduce_fusion.2
  259.5 48.3 %all-reduce = (f32[]{:T(128)}, f32[]{:T(128)}) all-reduce(f32[]{:T(128)S(6)} %add.78, f32[]{:T(128)S(6)} %add.81), channel_id=1, replica_groups=mesh['grp'=2,'cores'=16] {'grp','cores'}, use_global_device_ids=true, to_apply=%region_2.3 | all-reduce | flops 2 | bytes 16 | tf_op jit(solution)/shard_map/psum | solution.py:54
  311.8 38.3 %psum.60 = f32[]{:T(128)} all-reduce(f32[]{:T(128)S(6)} %add.82), channel_id=1, replica_groups=mesh['grp'=2,'cores'=16] {'grp','cores'}, use_global_device_ids=true, to_apply=%region_12.13 | all-reduce | flops 1 | bytes 8 | tf_op jit(solution)/shard_map/psum | solution.py:54
  351.5 4.6 fusion.10
  356.1 67.8 %all-reduce.4 = bf16[4,8192]{1,0:T(4,128)(2,1)S(1)} all-reduce(f32[4,8192]{1,0:T(4,128)S(1)} %fusion.10), channel_id=1, replica_groups=mesh['grp'=2,'cores'=16] {'cores'}, use_global_device_ids=true, to_apply=%region_13.14 | all-reduce | flops 32768 | bytes 196608 | tf_op jit(solution)/shard_map/psum | solution.py:12
  423.9 3.5 fusion.3
  428.1 1.9 copy.18
  430.1 78.8 %reduce-scatter.19.cloned.1.call-done = bf16[512,4]{1,0:T(8,128)(2,1)} async-done(((bf16[8192,4]{1,0:T(8,128)(2,1)}), bf16[512,4]{1,0:T(8,128)(2,1)}) %reduce-scatter.19.cloned.1.call-update) | async-done | bytes 4112
  509.8 2.5 psum.65
  512.3 4.6 convolution_convert_fusion
  516.9 1.9 copy.14
  519.5 77.7 %reduce-scatter.15.cloned.1.call-done = bf16[512,4]{1,0:T(8,128)(2,1)} async-done(((bf16[8192,4]{1,0:T(8,128)(2,1)}), bf16[512,4]{1,0:T(8,128)(2,1)}) %reduce-scatter.15.cloned.1.call-update) | async-done | bytes 4112
  597.2 1.7 multiply_reduce_fusion
  600.2 48.1 %psum.63 = f32[]{:T(128)} all-reduce(f32[]{:T(128)S(6)} %add.87), channel_id=1, replica_groups=mesh['grp'=2,'cores'=16] {'grp','cores'}, use_global_device_ids=true, to_apply=%region_19.20 | all-reduce | flops 1 | bytes 8 | tf_op jit(solution)/shard_map/psum | solution.py:62
  (39 shorter events, 8.9 us)
Async XLA Ops:
  7.2 0.7 copy-start
  7.2 159.7 %reduce-scatter.17.cloned.1.call-start = ((), (), s32[]{:S(2)}) async-start(), calls=%async_computation.6 | async-start | bytes 2228224
  9.3 72.5 %copy-start.5 = (f32[4,256]{1,0:T(4,128)S(1)}, f32[4,256]{1,0:T(4,128)}, u32[]{:S(2)}) copy-start(f32[4,256]{1,0:T(4,128)} %param.11) | copy-start | bytes 12292
  9.3 72.5 %copy-start.6 = (f32[4,256]{1,0:T(4,128)S(1)}, f32[4,256]{1,0:T(4,128)}, u32[]{:S(2)}) copy-start(f32[4,256]{1,0:T(4,128)} %param.9) | copy-start | bytes 12292
  9.3 72.5 %copy-start.7 = (f32[256]{0:T(256)S(1)}, f32[256]{0:T(256)}, u32[]{:S(2)}) copy-start(f32[256]{0:T(256)} %param.14) | copy-start | bytes 3076
  81.8 3.6 copy-start.1
  88.0 167.1 %reduce-scatter.13.cloned.1.call-start = ((), (), s32[]{:S(2)}) async-start(), calls=%async_computation.4 | async-start | bytes 2228224
  174.9 80.2 %copy-start.3 = (f32[4,512]{1,0:T(4,128)S(1)}, f32[4,512]{1,0:T(4,128)}, u32[]{:S(2)}) copy-start(f32[4,512]{1,0:T(4,128)} %param.10) | copy-start | bytes 24580
  174.9 80.2 %copy-start.4 = (f32[4,512]{1,0:T(4,128)S(1)}, f32[4,512]{1,0:T(4,128)}, u32[]{:S(2)}) copy-start(f32[4,512]{1,0:T(4,128)} %param.8) | copy-start | bytes 24580
  176.9 332.0 %reduce-scatter.19.cloned.1.call-start = ((), (), s32[]{:S(2)}) async-start(), calls=%async_computation.7 | async-start | bytes 2228224
  423.9 3.5 copy-start.2
  430.0 167.2 %reduce-scatter.15.cloned.1.call-start = ((), (), s32[]{:S(2)}) async-start(), calls=%async_computation.5 | async-start | bytes 2228224
Sparse Core Ops, SparseCore 0:
  88.2 78.6 reduce-scatter.16
  177.0 78.1 reduce-scatter.12
  430.1 78.6 reduce-scatter.18
  518.9 78.2 reduce-scatter.14
where the time goes:
time: 658 us; the launch traced here: 657 us
  waiting for transfers between devices  313 us (48%)
  blocking collectives  275 us (42%)
  matrix products  31.7 us (5%)
  between operations  23.1 us (4%)
  local copies, waits for them, and re-layouts  10.9 us (2%)
    unnamed x8, waiting for transfers between devices  313 us
    psum x2, blocking collectives, genomic_map(): mapped = lax.psum(partial_map, 'cores')  136 us
    psum x2, blocking collectives, residual_inner(): return lax.psum(local_sum, ('grp', 'cores'))  86.5 us
    psum x1, blocking collectives, body(): step_size = rz_now / lax.psum(local_curve, ('grp', 'cores'))  48.1 us
  transfers between devices with their start and end apart: 4, of which 4 were waited for; matrix products, arithmetic and copies ran while one was open for 0% of the time, Pallas kernels for 0%

commit v1 on v0

--- a/solution.py
+++ b/solution.py
@@ -9,7 +9,8 @@
 def genomic_map(core_vec, non_vec, core_inverse, genomic_block, m_inverse):
     core_in = core_vec.astype(jnp.bfloat16)
     partial_map = jnp.dot(core_in, core_inverse, preferred_element_type=jnp.float32)
-    mapped = lax.psum(partial_map, "cores")
+    parts = lax.all_gather(partial_map, "cores")
+    mapped = jnp.sum(parts, axis=0)
     mapped_in = mapped.astype(jnp.bfloat16)
     pulled = lax.dot_general(
         mapped_in, genomic_block, (((1,), (1,)), ((), ())), preferred_element_type=jnp.float32

time: 658 us -> 637 us (0.968)
  blocking collectives: 275 us -> 140 us
  waiting for transfers between devices: 313 us -> 421 us
    psum x2 -> x0, blocking collectives: 136 us -> none  [genomic_map(): mapped = lax.psum(partial_map, 'cores')]
    all_gather x0 -> x2, waiting for transfers between devices: none -> 123 us  [genomic_map(): parts = lax.all_gather(partial_map, 'cores')]
    unnamed x8 -> x10, waiting for transfers between devices: 313 us -> 298 us
  transfers between devices with their start and end apart: 4 -> 6, of which waited for: 4 -> 6; matrix products, arithmetic and copies ran while one was open for 0% -> 0% of each run, Pallas kernels for 0% -> 0%
where the time goes in v1:
time: 637 us; the launch traced here: 636 us
  waiting for transfers between devices  421 us (66%)
  blocking collectives  140 us (22%)
  matrix products  33 us (5%)
  between operations  23.4 us (4%)
  local copies, waits for them, and re-layouts  10.9 us (2%)
  other arithmetic  7.38 us (1%)
    unnamed x10, waiting for transfers between devices  298 us
    all_gather x2, waiting for transfers between devices, genomic_map(): parts = lax.all_gather(partial_map, 'cores')  123 us
    psum x2, blocking collectives, residual_inner(): return lax.psum(local_sum, ('grp', 'cores'))  86.5 us
    psum x1, blocking collectives, body(): step_size = rz_now / lax.psum(local_curve, ('grp', 'cores'))  48.3 us
  transfers between devices with their start and end apart: 6, of which 6 were waited for; matrix products, arithmetic and copies ran while one was open for 0% of the time, Pallas kernels for 0%

profile of v1, /device:TPU:12, one launch (start us, length us, event | category | flops | bytes accessed | tf_op | source)
XLA Modules:
  0.0 635.7 jit_solution(6201210966279950636)
XLA Ops:
  9.3 5.3 convolution_bitcast_fusion.1
  14.8 61.5 %all-gather.7.cloned.1.call-done = f32[16,4,8192]{2,1,0:T(4,128)} async-done(((f32[1,4,8192]{2,1,0:T(4,128)}), f32[16,4,8192]{2,1,0:T(4,128)}) %all-gather.7.cloned.1.call-update) | async-done | bytes 2097168 | tf_op jit(solution)/shard_map/all_gather | solution.py:12
  76.2 1.9 reduce_sum.92
  78.2 3.5 fusion.5
  82.4 1.9 copy.16
  84.3 71.3 %reduce-scatter.17.cloned.1.call-done = bf16[512,4]{1,0:T(8,128)(2,1)} async-done(((bf16[8192,4]{1,0:T(8,128)(2,1)}), bf16[512,4]{1,0:T(8,128)(2,1)}) %reduce-scatter.17.cloned.1.call-update) | async-done | bytes 4112
  156.6 2.5 psum.48
  159.1 4.6 convolution_convert_fusion.2
  163.6 1.9 copy.12
  166.4 77.7 %reduce-scatter.13.cloned.1.call-done = bf16[512,4]{1,0:T(8,128)(2,1)} async-done(((bf16[8192,4]{1,0:T(8,128)(2,1)}), bf16[512,4]{1,0:T(8,128)(2,1)}) %reduce-scatter.13.cloned.1.call-update) | async-done | bytes 4112
  244.1 1.7 multiply_reduce_fusion.2
  248.4 48.3 %all-reduce = (f32[]{:T(128)}, f32[]{:T(128)}) all-reduce(f32[]{:T(128)S(6)} %add.74, f32[]{:T(128)S(6)} %add.77), channel_id=1, replica_groups=mesh['grp'=2,'cores'=16] {'grp','cores'}, use_global_device_ids=true, to_apply=%region_2.3 | all-reduce | flops 2 | bytes 16 | tf_op jit(solution)/shard_map/psum | solution.py:55
  300.7 38.3 %psum.45 = f32[]{:T(128)} all-reduce(f32[]{:T(128)S(6)} %add.78), channel_id=1, replica_groups=mesh['grp'=2,'cores'=16] {'grp','cores'}, use_global_device_ids=true, to_apply=%region_12.13 | all-reduce | flops 1 | bytes 8 | tf_op jit(solution)/shard_map/psum | solution.py:55
  340.4 5.2 convolution_bitcast_fusion
  345.7 61.5 %all-gather.9.cloned.1.call-done = f32[16,4,8192]{2,1,0:T(4,128)} async-done(((f32[1,4,8192]{2,1,0:T(4,128)}), f32[16,4,8192]{2,1,0:T(4,128)}) %all-gather.9.cloned.1.call-update) | async-done | bytes 2097168 | tf_op jit(solution)/shard_map/all_gather | solution.py:12
  407.2 1.9 reduce_sum.97
  409.1 3.5 fusion.3
  413.3 1.9 copy.18
  415.3 71.3 %reduce-scatter.19.cloned.1.call-done = bf16[512,4]{1,0:T(8,128)(2,1)} async-done(((bf16[8192,4]{1,0:T(8,128)(2,1)}), bf16[512,4]{1,0:T(8,128)(2,1)}) %reduce-scatter.19.cloned.1.call-update) | async-done | bytes 4112
  487.5 2.5 psum.49
  490.0 4.6 convolution_convert_fusion
  494.6 1.9 copy.14
  497.2 77.8 %reduce-scatter.15.cloned.1.call-done = bf16[512,4]{1,0:T(8,128)(2,1)} async-done(((bf16[8192,4]{1,0:T(8,128)(2,1)}), bf16[512,4]{1,0:T(8,128)(2,1)}) %reduce-scatter.15.cloned.1.call-update) | async-done | bytes 4112
  578.0 48.3 %psum.47 = f32[]{:T(128)} all-reduce(f32[]{:T(128)S(6)} %add.83), channel_id=1, replica_groups=mesh['grp'=2,'cores'=16] {'grp','cores'}, use_global_device_ids=true, to_apply=%region_19.20 | all-reduce | flops 1 | bytes 8 | tf_op jit(solution)/shard_map/psum | solution.py:63
  (45 shorter events, 11.7 us)
Async XLA Ops:
  7.2 0.7 copy-start
  7.2 69.0 %all-gather.7.cloned.1.call-start = ((), (), s32[]{:S(2)}) async-start(), calls=%async_computation.4 | async-start | bytes 2228224 | tf_op jit(solution)/shard_map/all_gather | solution.py:12
  9.3 5.4 copy-start.5
  9.3 5.4 copy-start.6
  9.3 5.4 copy-start.7
  14.6 141.0 %reduce-scatter.17.cloned.1.call-start = ((), (), s32[]{:S(2)}) async-start(), calls=%async_computation.8 | async-start | bytes 2228224
  78.1 3.5 copy-start.1
  84.3 159.8 %reduce-scatter.13.cloned.1.call-start = ((), (), s32[]{:S(2)}) async-start(), calls=%async_computation.6 | async-start | bytes 2228224
  163.6 80.5 %copy-start.3 = (f32[4,512]{1,0:T(4,128)S(1)}, f32[4,512]{1,0:T(4,128)}, u32[]{:S(2)}) copy-start(f32[4,512]{1,0:T(4,128)} %param.10) | copy-start | bytes 24580
  163.6 80.5 %copy-start.4 = (f32[4,512]{1,0:T(4,128)S(1)}, f32[4,512]{1,0:T(4,128)}, u32[]{:S(2)}) copy-start(f32[4,512]{1,0:T(4,128)} %param.8) | copy-start | bytes 24580
  165.6 241.6 %all-gather.9.cloned.1.call-start = ((), (), s32[]{:S(2)}) async-start(), calls=%async_computation.5 | async-start | bytes 2228224 | tf_op jit(solution)/shard_map/all_gather | solution.py:12
  345.6 140.9 %reduce-scatter.19.cloned.1.call-start = ((), (), s32[]{:S(2)}) async-start(), calls=%async_computation.9 | async-start | bytes 2228224
  409.1 3.5 copy-start.2
  415.2 159.8 %reduce-scatter.15.cloned.1.call-start = ((), (), s32[]{:S(2)}) async-start(), calls=%async_computation.7 | async-start | bytes 2228224
Sparse Core Ops, SparseCore 0:
  14.7 61.4 all-gather.6
  84.4 71.1 reduce-scatter.16
  165.7 78.3 reduce-scatter.12
  345.7 61.3 all-gather.8
  415.3 71.1 reduce-scatter.18
  496.6 78.3 reduce-scatter.14
